TPU v7x, 256 devices: a whole 4x4x8 slice. The times are simulated.
256 devices in a mesh: seq: 16 (over x, y), fsdp: 16 (over z, core).
Axes of the slice: x: 4, y: 4, z: 8, core: 2. Of those that a mesh axis runs over, the one named last changes fastest.
Arguments:
- patches: bfloat16 [16, 8704, 1176], P('fsdp', 'seq'), may hold values from -6 to 6
- send_slot: int32 [16, 272], P('fsdp', 'seq'), may hold values from 0 to 271, as said below
- segments: int32 [16, 272], P('fsdp'), may hold values from 0 to 33, never falling along the last dimension, each value on 1 to 24 neighbouring positions
- stem_weight: bfloat16 [3584, 1176], P('fsdp'), may hold values from -0.1875 to 0.1875
- norm_gain: bfloat16 [3584], P('fsdp'), may hold values from 0.099609375 to 1.8984375
- conv_kernel: bfloat16 [5, 3584], P(None, 'fsdp'), may hold values from -3 to 3
- cotangent: bfloat16 [16, 8704, 3584], P('fsdp', 'seq'), may hold values from -6 to 6
Outputs:
- features: bfloat16 [16, 8704, 3584], P('fsdp', 'seq')
- grad_patches: bfloat16 [16, 8704, 1176], P('fsdp', 'seq')
- grad_weight: bfloat16 [3584, 1176], P('fsdp')
- grad_channels: float32 [6, 3584], P(None, 'fsdp')
Inputs may be any that keep to these rules, and one draw needn't show every extreme that they name: `send_slot`: each row is a permutation of the packed slots. At most 2 frame slots of one device go to one device's packed slots, and every device sends exactly 2 to some device; within a row the number that device s sends to device (s + o) modulo the seq axis size depends on o alone. `segments`: ids never fall along a row; a clip holds 1 to 24 slots, one exactly 24.
All inputs are finite; a program needn't handle non-finite values.
Results may differ from a plain program's by a relative error of at most 0.0056.
Values may be sent and summed in bfloat16 or wider, within the bound.
A program may use at most 192 MiB of HBM per device.

v0:
```python
import math
import jax
import jax.numpy as jnp
from jax import lax
from jax.sharding import PartitionSpec as P

EPSILON = 1e-06


def pl_ceil(total, step):
    return -(-total // step)


def extended_2(cells, sides, width):
    for axis, dim in sides:
        count = lax.axis_size(axis)
        ends = count - 1
        head = lax.slice_in_dim(cells, 0, width, axis=dim)
        tail = lax.slice_in_dim(cells, cells.shape[dim] - width, cells.shape[dim], axis=dim)
        cells = jnp.concatenate(
            [
                lax.ppermute(tail, axis, [(i, (i + 1) % count) for i in range(ends)]),
                cells,
                lax.ppermute(head, axis, [((i + 1) % count, i) for i in range(ends)]),
            ],
            axis=dim,
        )
    return cells


def slot_mask(segment_row, centre):
    slot_total = segment_row.shape[0]
    safe_centre = jnp.clip(centre, 0, slot_total - 1)
    columns = []
    for offset in range(5):
        neighbour = centre + (offset - 2)
        inside = (neighbour >= 0) & (neighbour < slot_total) & (centre >= 0) & (centre < slot_total)
        same_clip = segment_row[jnp.clip(neighbour, 0, slot_total - 1)] == segment_row[safe_centre]
        columns.append((inside & same_clip).astype(jnp.float32))
    return jnp.stack(columns, axis=1)


def temporal_mix(padded, clip_mask, kernel, slot_total):
    kernel_wide = kernel.astype(jnp.float32)
    result = padded[0:slot_total].astype(jnp.float32) * (
        clip_mask[:, 0][:, None, None] * kernel_wide[0][None, None, :]
    )
    for offset in range(1, 5):
        addend = padded[offset : offset + slot_total].astype(jnp.float32) * (
            clip_mask[:, offset][:, None, None] * kernel_wide[offset][None, None, :]
        )
        result = result + addend
    return result


def temporal_back(slope_padded, mask_padded, kernel, slot_total):
    kernel_wide = kernel.astype(jnp.float32)
    result = jnp.zeros((slot_total,) + slope_padded.shape[1:], jnp.float32)
    for offset in range(5):
        first_row = 4 - offset
        weights_row = (
            mask_padded[first_row : first_row + slot_total, offset][:, None, None]
            * kernel_wide[offset][None, None, :]
        )
        result = (
            result
            + slope_padded[first_row : first_row + slot_total].astype(jnp.float32) * weights_row
        )
    return result


def kernel_sums(slope_blocks, padded, clip_mask, slot_total):
    stacked = []
    for offset in range(5):
        product = jnp.sum(
            slope_blocks.astype(jnp.float32)
            * padded[offset : offset + slot_total].astype(jnp.float32),
            axis=1,
        )
        stacked.append(jnp.sum(product * clip_mask[:, offset][:, None], axis=0))
    return jnp.stack(stacked, axis=0)


def rim_rows(values, margin):
    return extended_2(values, (("seq", 0),), margin)


def shards(patches, send_slot, segments, stem_weight, norm_gain, conv_kernel, cotangent):
    seq_size = lax.axis_size("seq")
    fsdp_size = lax.axis_size("fsdp")
    seq_index = lax.axis_index("seq")
    slot_count = send_slot.shape[1]
    tokens = patches.shape[1]
    slot_rows = tokens // slot_count
    pixel_width = patches.shape[2]
    capacity = 2 * slot_count // seq_size
    destination = send_slot[0]
    owner_index = destination // slot_count
    same_owner = owner_index[:, None] == owner_index[None, :]
    earlier = destination[None, :] < destination[:, None]
    ranking = jnp.sum((same_owner & earlier).astype(jnp.int32), axis=1)
    buffer_row = owner_index * capacity + ranking
    frames = patches[0].reshape(slot_count, slot_rows, pixel_width)
    outbox = (
        jnp.zeros((seq_size * capacity, slot_rows, pixel_width), jnp.bfloat16)
        .at[buffer_row]
        .set(frames)
    )
    position = (
        jnp.full((seq_size * capacity,), -1.0, jnp.float32)
        .at[buffer_row]
        .set((destination % slot_count).astype(jnp.float32))
        .astype(jnp.bfloat16)
    )
    incoming, arrived = (
        lax.all_to_all(outbox, "seq", split_axis=0, concat_axis=0, tiled=True),
        lax.all_to_all(position, "seq", split_axis=0, concat_axis=0, tiled=True),
    )
    arrived_float = arrived.astype(jnp.float32)
    target = jnp.where(arrived_float >= 0.0, arrived_float, float(slot_count)).astype(jnp.int32)
    packed = (
        jnp.zeros((slot_count + 1, slot_rows, pixel_width), jnp.bfloat16)
        .at[target]
        .set(incoming)[:slot_count]
        .reshape(tokens, pixel_width)
    )
    extras = jnp.concatenate([norm_gain[:, None], conv_kernel.T], axis=1)
    shard_ext = jnp.concatenate([stem_weight, extras], axis=1)
    gathered = lax.all_gather(shard_ext, "fsdp", axis=0, tiled=True)
    weight_full = gathered[:, :pixel_width]
    channel_low = gathered[:, pixel_width:].T
    gain_low = channel_low[0]
    kernel_full = channel_low[1:]
    gain_wide = gain_low.astype(jnp.float32)
    channels = weight_full.shape[0]
    stem_out = lax.dot_general(
        packed, weight_full, (((1,), (1,)), ((), ())), preferred_element_type=jnp.float32
    )
    inv_rms = lax.rsqrt(jnp.mean(stem_out * stem_out, axis=1, keepdims=True) + EPSILON)
    unit_rows = stem_out * inv_rms
    normed = (unit_rows * gain_wide).astype(jnp.bfloat16)
    segment_row = segments[0]
    centre = seq_index * slot_count + jnp.arange(slot_count, dtype=jnp.int32)
    extended = seq_index * slot_count + jnp.arange(-2, slot_count + 2, dtype=jnp.int32)
    clip_mask = slot_mask(segment_row, centre)
    mask_padded = slot_mask(segment_row, extended)
    padded = rim_rows(normed, 2 * slot_rows).reshape(slot_count + 4, slot_rows, channels)
    mixed_rows = temporal_mix(padded, clip_mask, kernel_full, slot_count).reshape(tokens, channels)
    features = (stem_out + jax.nn.silu(mixed_rows)).astype(jnp.bfloat16)
    upstream_wide = cotangent[0].astype(jnp.float32)
    gate_value = jax.nn.sigmoid(mixed_rows)
    slope_low = (upstream_wide * gate_value * (1.0 + mixed_rows * (1.0 - gate_value))).astype(
        jnp.bfloat16
    )
    slope_padded = rim_rows(slope_low, 2 * slot_rows).reshape(slot_count + 4, slot_rows, channels)
    d_normed = temporal_back(slope_padded, mask_padded, kernel_full, slot_count).reshape(
        tokens, channels
    )
    gated = d_normed * gain_wide
    d_stem = upstream_wide + inv_rms * (
        gated - unit_rows * jnp.mean(gated * unit_rows, axis=1, keepdims=True)
    )
    d_stem_low = d_stem.astype(jnp.bfloat16)
    grad_rows = jnp.dot(d_stem_low, weight_full, preferred_element_type=jnp.float32).astype(
        jnp.bfloat16
    )
    gain_part = jnp.sum(d_normed * unit_rows, axis=0)
    slope_blocks = slope_padded[2 : 2 + slot_count]
    kernel_part = kernel_sums(slope_blocks, padded, clip_mask, slot_count)
    chan_terms = jnp.concatenate([gain_part[None, :], kernel_part], axis=0).T
    weight_block = lax.dot_general(
        d_stem_low,
        jnp.pad(packed, ((0, 0), (0, 6))),
        (((0,), (0,)), ((), ())),
        preferred_element_type=jnp.float32,
    )
    total_block = weight_block + jnp.pad(chan_terms, ((0, 0), (pixel_width, 0)))
    panel = channels // fsdp_size
    panel_padded = 16 * seq_size * pl_ceil(panel, 16 * seq_size)
    stacked = jnp.pad(
        total_block.reshape(fsdp_size, panel, pixel_width + 6),
        ((0, 0), (0, panel_padded - panel), (0, 0)),
    ).reshape(fsdp_size * panel_padded, pixel_width + 6)
    piece = lax.psum_scatter(stacked, ("fsdp", "seq"), scatter_dimension=0, tiled=True)
    grad_scale = 1.0 / math.sqrt(tokens * seq_size * fsdp_size)
    summed = lax.all_gather(piece * grad_scale, "seq", axis=0, tiled=True)[:panel]
    grad_weight = summed[:, :pixel_width].astype(jnp.bfloat16)
    grad_channels = summed[:, pixel_width:].T
    return (features[None], grad_rows[None], grad_weight, grad_channels)


def solution(mesh):
    in_specs = (
        P("fsdp", "seq", None),
        P("fsdp", "seq"),
        P("fsdp", None),
        P("fsdp", None),
        P("fsdp"),
        P(None, "fsdp"),
        P("fsdp", "seq", None),
    )
    out_specs = (P("fsdp", "seq", None), P("fsdp", "seq", None), P("fsdp", None), P(None, "fsdp"))
    return jax.shard_map(shards, mesh=mesh, in_specs=in_specs, out_specs=out_specs, check_vma=False)
```

profile of v0, /device:TPU:1, one launch (start us, length us, event | category | flops | bytes accessed | tf_op | source)
XLA Modules:
  0.0 1608.6 jit_solution(15183071175365913867)
XLA Ops:
  7.2 0.7 broadcast_in_dim.26
  8.0 0.8 copy.34
  8.8 1.9 concatenate.24
  10.7 0.7 fusion.30
  11.4 0.7 fusion.31
  12.1 0.9 convert_reduce_fusion.1
  13.0 0.7 fusion.34
  13.7 0.6 scatter_custom_fusion
  14.3 0.7 all_to_all.12
  15.0 7.6 all-to-all-start
  22.8 1.8 broadcast_in_dim.21
  24.6 7.2 scatter_fusion
  31.9 6.7 all-to-all-start.1
  38.6 0.7 gather_fusion
  39.4 0.7 gather_fusion.5
  40.1 0.7 gather_fusion.1
  40.8 0.7 gather_fusion.2
  41.5 0.7 gather_fusion.3
  42.2 0.7 gather_fusion.4
  42.9 0.7 gather_fusion.7
  43.6 0.7 gather_fusion.6
  44.3 0.7 gather_fusion.8
  45.1 0.7 gather_fusion.9
  46.3 26.7 %all-to-all-done.1 = bf16[32,32,1176]{2,1,0:T(8,128)(2,1)} async-done(((bf16[32,32,1176]{2,1,0:T(8,128)(2,1)}), bf16[32,32,1176]{2,1,0:T(8,128)(2,1)}, u32[]{:S(2)}, u32[]{:S(2)}) %all-to-all-start.1) | async-done | bytes 2408480 | tf_op jit(solution)/shard_map/all_to_all | solution.py:116
  73.0 0.1 broadcast_in_dim.18
  73.1 4.6 scatter_fusion.1
  77.9 1.6 slice_bitcast_fusion
  79.5 0.3 convert_reduce_fusion
  79.9 0.3 slice_convert_fusion.1
  80.2 4.3 slice_reduce_fusion.4
  84.5 5.5 multiply_reduce_fusion.2
  90.0 1.3 multiply_convert_fusion
  91.4 2.6 collective-permute-start
  94.0 1.4 collective-permute-start.1
  95.6 0.8 broadcast_multiply_fusion
  96.4 0.9 broadcast_multiply_fusion.1
  97.3 0.9 broadcast_multiply_fusion.2
  98.2 0.9 broadcast_multiply_fusion.3
  99.0 1.4 collective-permute-done
  100.4 4.1 collective-permute-done.1
  104.6 19.6 %convert_multiply_fusion = (f32[544,3584]{1,0:T(8,128)}, bf16[544,3584]{1,0:T(8,128)(2,1)}, f32[544,3584]{1,0:T(8,128)}) fusion(bf16[64,3584]{1,0:T(8,128)(2,1)S(1)} %collective-permute-done.1, bf16[544,3584]{1,0:T(8,128)(2,1)S(1)} %multiply_convert_fusion, bf16[1,544,3584]{2,1,0:T(8,128)(2,1)S(1)} %copy-done.4, f32[17,3584]{1,0:T(8,128)S(1)} %get-tuple-element.57, ...), kind=kLoop, calls=%fused_computation.13 | loop fusion | flops 74088448 | bytes 29431808 | tf_op jit(solution)/shard_map/mul | solution.py:76
  124.2 4.3 reduce_sum.141
  128.7 2.0 fusion.54
  130.7 1.3 collective-permute-start.2
  131.9 4.8 collective-permute-start.3
  136.8 15.1 convert_multiply_fusion.1
  151.9 4.3 reduce_sum.139
  156.4 4.4 reduce_sum.137
  160.9 4.4 reduce_sum.133
  165.4 4.4 reduce_sum.135
  169.9 10.2 fusion.13
  180.2 2.1 multiply_reduce_fusion
  182.3 9.6 fusion.10
  192.0 0.1 concatenate.29
  192.1 13.7 pad_add_fusion
  205.8 18.8 %copy.35 = f32[3584,1182]{1,0:T(8,128)} copy(f32[3584,1182]{0,1:T(8,128)} %pad_add_fusion) | data formatting | bytes 33890304 | tf_op jit(solution)/shard_map/add | solution.py:177
  224.6 15.3 pad.14
  239.9 1284.5 %reduce-scatter.4.cloned.1.call-done = f32[16,1182]{1,0:T(8,128)} async-done(((f32[4096,1182]{1,0:T(8,128)}), f32[16,1182]{1,0:T(8,128)}) %reduce-scatter.4.cloned.1.call-update) | async-done | bytes 75664 | tf_op jit(solution)/shard_map/reduce_scatter | solution.py:184
  1524.4 1.5 broadcast_multiply_fusion.10
  1526.0 10.4 fusion.23
  1536.4 61.6 %all-gather.5.cloned.1.call-done = f32[256,1182]{1,0:T(8,128)} async-done(((f32[16,1182]{1,0:T(8,128)}), f32[256,1182]{1,0:T(8,128)}) %all-gather.5.cloned.1.call-update) | async-done | bytes 1210384 | tf_op jit(solution)/shard_map/all_gather | solution.py:186
  1598.0 1.0 slice_bitcast_fusion.1
  1599.0 0.7 copy.38
  1599.7 2.1 slice.292
  (75 shorter events, 1.8 us)
Async XLA Ops:
  7.2 31.5 %copy-start = (s32[1,272]{1,0:T(1,128)S(1)}, s32[1,272]{1,0:T(1,128)}, u32[]{:S(2)}) copy-start(s32[1,272]{1,0:T(1,128)} %param.9) | copy-start | bytes 3268
  7.2 70.7 %all-gather.3.cloned.1.call-start = ((), (), s32[]{:S(2)}) async-start(), calls=%async_computation.3 | async-start | bytes 9748480 | tf_op jit(solution)/shard_map/all_gather | solution.py:129
  15.0 16.9 %all-to-all-start = ((bf16[16,2,1]{1,2,0:T(2,128)(2,1)}), bf16[16,2,1]{1,2,0:T(2,128)(2,1)S(1)}, u32[]{:S(2)}, u32[]{:S(2)}) async-start(bf16[16,2,1]{1,2,0:T(2,128)(2,1)} %all_to_all.12), calls=%async_computation | async-start | bytes 16384 | tf_op jit(solution)/shard_map/all_to_all | solution.py:117
  31.9 41.1 %all-to-all-start.1 = ((bf16[32,32,1176]{2,1,0:T(8,128)(2,1)}), bf16[32,32,1176]{2,1,0:T(8,128)(2,1)}, u32[]{:S(2)}, u32[]{:S(2)}) async-start(bf16[32,32,1176]{2,1,0:T(8,128)(2,1)} %scatter_fusion), calls=%async_computation.1 | async-start | bytes 5242880 | tf_op jit(solution)/shard_map/all_to_all | solution.py:116
  38.5 1485.8 %reduce-scatter.4.cloned.1.call-start = ((), (), s32[]{:S(2)}) async-start(), calls=%async_computation.5 | async-start | bytes 21053440 | tf_op jit(solution)/shard_map/reduce_scatter | solution.py:184
  77.9 6.7 copy-start.5
  90.0 7.3 copy-start.2
  90.0 14.6 copy-start.4
  91.3 32.8 %copy-start.3 = (bf16[544,3584]{1,0:T(8,128)(2,1)}, bf16[544,3584]{1,0:T(8,128)(2,1)S(1)}, u32[]{:S(2)}) copy-start(bf16[544,3584]{1,0:T(8,128)(2,1)S(1)} %multiply_convert_fusion) | copy-start | bytes 11698180
  91.4 9.0 collective-permute-start
  94.0 10.5 collective-permute-start.1
  130.7 39.3 %collective-permute-start.2 = (bf16[64,3584]{1,0:T(8,128)(2,1)}, bf16[64,3584]{1,0:T(8,128)(2,1)}, u32[]{:S(2)}, u32[]{:S(2)}) collective-permute-start(bf16[64,3584]{1,0:T(8,128)(2,1)} %get-tuple-element.44), channel_id=1, source_target_pairs={{16,0},{32,16},{48,32},{64,48},{80,64},{96,80},{112,96},{128,112},... | collective-permute-start | bytes 1376264 | tf_op jit(solution)/shard_map/ppermute | solution.py:24
  131.9 38.0 %collective-permute-start.3 = (bf16[64,3584]{1,0:T(8,128)(2,1)S(1)}, bf16[64,3584]{1,0:T(8,128)(2,1)}, u32[]{:S(2)}, u32[]{:S(2)}) collective-permute-start(bf16[64,3584]{1,0:T(8,128)(2,1)S(1)} %get-tuple-element.45), channel_id=1, source_target_pairs={{0,16},{16,32},{32,48},{48,64},{64,80},{80,96},{96,112},{112,128},... | collective-permute-start | bytes 1376264 | tf_op jit(solution)/shard_map/ppermute | solution.py:22
  169.8 10.4 slice-start
  169.9 10.3 slice-start.1
  239.9 1358.1 %all-gather.5.cloned.1.call-start = ((), (), s32[]{:S(2)}) async-start(), calls=%async_computation.4 | async-start | bytes 1392640 | tf_op jit(solution)/shard_map/all_gather | solution.py:186
  1526.0 75.9 %copy-start.1 = (s32[1,272]{1,0:T(1,128)S(1)}, s32[1,272]{1,0:T(1,128)}, u32[]{:S(2)}) copy-start(s32[1,272]{1,0:T(1,128)} %param.9) | copy-start | bytes 3268
Sparse Core Ops, SparseCore 0:
  10.9 63.8 all-gather.2
  240.0 1284.3 reduce-scatter.3
  1527.5 70.5 all-gather.4
where the time goes:
time: 1610 us
  waiting for transfers between devices  1380 us (86%)
  other arithmetic  89.6 us (6%)
  local copies, waits for them, and re-layouts  72 us (4%)
  matrix products  29.6 us (2%)
  starting transfers between devices  24.5 us (2%)
    reduce_scatter x1, waiting for transfers between devices, shards(): lax.psum_scatter(stacked, ('fsdp', 'seq'), scatter_dimension=0, tiled=True)  1280 us
    all_gather x1, waiting for transfers between devices, shards(): lax.all_gather(piece * grad_scale, 'seq', axis=0, tiled=True)[:panel]  61.6 us
    mul x2, other arithmetic, kernel_sums(): slope_blocks.astype(jnp.float32)  34.7 us
  transfers between devices with their start and end apart: 9, of which 5 were waited for; matrix products, arithmetic and copies ran while one was open for 4% of the time, Pallas kernels for 0%

commit v1 on v0

--- a/solution.py
+++ b/solution.py
@@ -5,6 +5,28 @@
 from jax.sharding import PartitionSpec as P
 
 EPSILON = 1e-06
+
+
+def in_order(blocks, dim):
+    blocks = jnp.moveaxis(blocks, 0, dim)
+    shape = blocks.shape
+    return blocks.reshape(*shape[:dim], shape[dim] * shape[dim + 1], *shape[dim + 2 :])
+
+
+def gather_around(x, axis, dim):
+    size = lax.axis_size(axis)
+    pairs = [(i, (i + 1) % size) for i in range(size)]
+    back = [(b, a) for a, b in pairs]
+    lower, upper = ([], [])
+    for step in range(size - 1):
+        if step % 2 == 0:
+            lower.append(lax.ppermute(lower[-1] if lower else x, axis, pairs))
+        else:
+            upper.append(lax.ppermute(upper[-1] if upper else x, axis, back))
+    parts = jnp.stack([*lower[::-1], x, *upper])
+    shift = lax.axis_index(axis) - len(lower)
+    parts = parts[(jnp.arange(size) - shift) % size]
+    return in_order(parts, dim)
 
 
 def pl_ceil(total, step):
@@ -183,7 +205,7 @@
     ).reshape(fsdp_size * panel_padded, pixel_width + 6)
     piece = lax.psum_scatter(stacked, ("fsdp", "seq"), scatter_dimension=0, tiled=True)
     grad_scale = 1.0 / math.sqrt(tokens * seq_size * fsdp_size)
-    summed = lax.all_gather(piece * grad_scale, "seq", axis=0, tiled=True)[:panel]
+    summed = gather_around(piece * grad_scale, "seq", 0)[:panel]
     grad_weight = summed[:, :pixel_width].astype(jnp.bfloat16)
     grad_channels = summed[:, pixel_width:].T
     return (features[None], grad_rows[None], grad_weight, grad_channels)

time: 1610 us -> 1630 us (1.012)
  the two profiles are of different devices: /device:TPU:1 before, /device:TPU:30 now
where the time goes in v1:
time: 1630 us
  waiting for transfers between devices  1330 us (82%)
  starting transfers between devices  105 us (6%)
  other arithmetic  79.6 us (5%)
  local copies, waits for them, and re-layouts  70.4 us (4%)
  matrix products  29.6 us (2%)
    reduce_scatter x1, waiting for transfers between devices, shards(): lax.psum_scatter(stacked, ('fsdp', 'seq'), scatter_dimension=0, tiled=True)  1280 us
    ppermute x8, starting transfers between devices, gather_around(): lower.append(lax.ppermute(lower[-1] if lower else x, axis, pairs))  77.7 us
  transfers between devices with their start and end apart: 23, of which 14 were waited for; matrix products, arithmetic and copies ran while one was open for 4% of the time, Pallas kernels for 0%

profile of v1, /device:TPU:30, one launch (start us, length us, event | category | flops | bytes accessed | tf_op | source)
XLA Modules:
  0.0 1627.9 jit_solution(6168049221587742807)
XLA Ops:
  7.2 0.7 broadcast_in_dim.26
  8.0 0.8 copy.24
  8.8 1.9 concatenate.24
  12.1 0.9 convert_reduce_fusion.1
  15.0 7.1 all-to-all-start
  22.3 1.8 broadcast_in_dim.21
  24.1 6.9 scatter_fusion
  31.0 7.2 all-to-all-start.1
  39.0 0.7 gather_fusion.5
  39.7 0.7 gather_fusion.1
  40.5 0.7 gather_fusion.2
  41.2 0.7 gather_fusion.3
  41.9 0.7 gather_fusion.4
  44.0 0.7 gather_fusion.8
  45.9 23.6 %all-to-all-done.1 = bf16[32,32,1176]{2,1,0:T(8,128)(2,1)} async-done(((bf16[32,32,1176]{2,1,0:T(8,128)(2,1)}), bf16[32,32,1176]{2,1,0:T(8,128)(2,1)}, u32[]{:S(2)}, u32[]{:S(2)}) %all-to-all-start.1) | async-done | bytes 2408480 | tf_op jit(solution)/shard_map/all_to_all | solution.py:138
  69.7 4.7 scatter_fusion.1
  74.5 1.6 slice_bitcast_fusion
  76.8 4.3 slice_reduce_fusion.4
  81.2 5.5 multiply_reduce_fusion.2
  86.7 1.3 multiply_convert_fusion
  88.1 1.6 collective-permute-start
  89.6 4.7 collective-permute-start.1
  94.5 0.8 broadcast_multiply_fusion
  95.3 0.9 broadcast_multiply_fusion.1
  96.2 0.9 broadcast_multiply_fusion.2
  97.1 0.9 broadcast_multiply_fusion.3
  97.9 3.7 collective-permute-done
  101.6 1.2 collective-permute-done.1
  102.8 10.2 convert_multiply_fusion
  113.1 4.3 reduce_sum.141
  117.6 2.0 fusion.56
  119.5 5.2 collective-permute-start.2
  124.7 1.3 collective-permute-start.3
  126.0 15.1 convert_multiply_fusion.1
  141.1 4.3 reduce_sum.139
  145.6 4.4 reduce_sum.137
  150.1 4.4 reduce_sum.133
  154.6 4.4 reduce_sum.135
  159.2 10.2 fusion.13
  169.5 2.1 multiply_reduce_fusion
  171.6 9.6 fusion.10
  181.3 13.7 pad_add_fusion
  195.1 18.8 %copy.25 = f32[3584,1182]{1,0:T(8,128)} copy(f32[3584,1182]{0,1:T(8,128)} %pad_add_fusion) | data formatting | bytes 33890304 | tf_op jit(solution)/shard_map/add | solution.py:199
  213.9 15.3 pad.14
  229.1 1277.6 %reduce-scatter.2.cloned.1.call-done = f32[16,1182]{1,0:T(8,128)} async-done(((f32[4096,1182]{1,0:T(8,128)}), f32[16,1182]{1,0:T(8,128)}) %reduce-scatter.2.cloned.1.call-update) | async-done | bytes 75664 | tf_op jit(solution)/shard_map/reduce_scatter | solution.py:206
  1506.7 0.9 broadcast_multiply_fusion.10
  1507.6 37.4 %collective-permute-start.4 = (f32[16,1182]{1,0:T(8,128)S(1)}, f32[16,1182]{1,0:T(8,128)S(1)}, u32[]{:S(2)}, u32[]{:S(2)}) collective-permute-start(f32[16,1182]{1,0:T(8,128)S(1)} %broadcast_multiply_fusion.10), channel_id=1, source_target_pairs={{0,16},{16,32},{32,48},{48,64},{64,80},{80,96},{96,112},{112,128},... | collective-permute-start | bytes 226952 | tf_op jit(solution)/shard_map/ppermute | solution.py:23
  1545.0 2.1 collective-permute-done.4
  1547.1 5.7 collective-permute-start.5
  1552.8 2.3 collective-permute-done.5
  1555.1 5.8 collective-permute-start.6
  1561.1 2.0 collective-permute-done.6
  1563.1 5.8 collective-permute-start.7
  1568.9 2.1 collective-permute-done.7
  1571.0 5.7 collective-permute-start.8
  1576.7 2.1 collective-permute-done.8
  1578.7 5.9 collective-permute-start.9
  1584.8 1.9 collective-permute-done.9
  1586.7 5.7 collective-permute-start.10
  1592.5 2.0 collective-permute-done.10
  1594.5 5.7 collective-permute-start.11
  1600.2 10.4 fusion.23
  1610.9 7.5 collective-permute-done.18
  1619.2 0.9 slice.300
  (124 shorter events, 10.9 us)
Async XLA Ops:
  7.2 31.1 %copy-start = (s32[1,272]{1,0:T(1,128)S(1)}, s32[1,272]{1,0:T(1,128)}, u32[]{:S(2)}) copy-start(s32[1,272]{1,0:T(1,128)} %param.9) | copy-start | bytes 3268
  7.2 67.3 %all-gather.2.cloned.1.call-start = ((), (), s32[]{:S(2)}) async-start(), calls=%async_computation.3 | async-start | bytes 9748480 | tf_op jit(solution)/shard_map/all_gather | solution.py:151
  15.0 16.0 all-to-all-start
  31.0 38.5 %all-to-all-start.1 = ((bf16[32,32,1176]{2,1,0:T(8,128)(2,1)}), bf16[32,32,1176]{2,1,0:T(8,128)(2,1)}, u32[]{:S(2)}, u32[]{:S(2)}) async-start(bf16[32,32,1176]{2,1,0:T(8,128)(2,1)} %scatter_fusion), calls=%async_computation.1 | async-start | bytes 5242880 | tf_op jit(solution)/shard_map/all_to_all | solution.py:138
  38.2 1468.5 %reduce-scatter.2.cloned.1.call-start = ((), (), s32[]{:S(2)}) async-start(), calls=%async_computation.4 | async-start | bytes 21053440 | tf_op jit(solution)/shard_map/reduce_scatter | solution.py:206
  74.5 6.7 copy-start.6
  86.6 9.5 copy-start.2
  86.7 16.2 copy-start.4
  88.0 25.1 %copy-start.3 = (bf16[544,3584]{1,0:T(8,128)(2,1)}, bf16[544,3584]{1,0:T(8,128)(2,1)S(1)}, u32[]{:S(2)}) copy-start(bf16[544,3584]{1,0:T(8,128)(2,1)S(1)} %multiply_convert_fusion) | copy-start | bytes 11698180
  88.1 13.6 collective-permute-start
  89.6 13.2 collective-permute-start.1
  119.5 39.6 %collective-permute-start.2 = (bf16[64,3584]{1,0:T(8,128)(2,1)}, bf16[64,3584]{1,0:T(8,128)(2,1)}, u32[]{:S(2)}, u32[]{:S(2)}) collective-permute-start(bf16[64,3584]{1,0:T(8,128)(2,1)} %get-tuple-element.40), channel_id=1, source_target_pairs={{16,0},{32,16},{48,32},{64,48},{80,64},{96,80},{112,96},{128,112},... | collective-permute-start | bytes 1376264 | tf_op jit(solution)/shard_map/ppermute | solution.py:46
  124.7 34.5 %collective-permute-start.3 = (bf16[64,3584]{1,0:T(8,128)(2,1)S(1)}, bf16[64,3584]{1,0:T(8,128)(2,1)}, u32[]{:S(2)}, u32[]{:S(2)}) collective-permute-start(bf16[64,3584]{1,0:T(8,128)(2,1)S(1)} %get-tuple-element.41), channel_id=1, source_target_pairs={{0,16},{16,32},{32,48},{48,64},{64,80},{80,96},{96,112},{112,128},... | collective-permute-start | bytes 1376264 | tf_op jit(solution)/shard_map/ppermute | solution.py:44
  159.0 10.4 slice-start
  159.2 10.3 slice-start.1
  1507.6 39.4 %collective-permute-start.4 = (f32[16,1182]{1,0:T(8,128)S(1)}, f32[16,1182]{1,0:T(8,128)S(1)}, u32[]{:S(2)}, u32[]{:S(2)}) collective-permute-start(f32[16,1182]{1,0:T(8,128)S(1)} %broadcast_multiply_fusion.10), channel_id=1, source_target_pairs={{0,16},{16,32},{32,48},{48,64},{64,80},{80,96},{96,112},{112,128},... | collective-permute-start | bytes 226952 | tf_op jit(solution)/shard_map/ppermute | solution.py:23
  1547.1 8.0 collective-permute-start.5
  1552.8 8.3 collective-permute-start.12
  1555.1 8.0 collective-permute-start.6
  1561.1 7.8 collective-permute-start.13
  1563.1 7.9 collective-permute-start.7
  1568.9 7.8 collective-permute-start.14
  1571.0 7.8 collective-permute-start.8
  1576.7 8.0 collective-permute-start.15
  1578.7 8.0 collective-permute-start.9
  1584.7 7.8 collective-permute-start.16
  1586.7 7.8 collective-permute-start.10
  1592.4 18.3 %copy-start.5 = (f32[16,1182]{1,0:T(8,128)S(1)}, f32[16,1182]{1,0:T(8,128)}, u32[]{:S(2)}) copy-start(f32[16,1182]{1,0:T(8,128)} %reduce-scatter.2.cloned.1.call-done) | copy-start | bytes 226948
  1592.5 18.1 %collective-permute-start.17 = (f32[16,1182]{1,0:T(8,128)S(1)}, f32[16,1182]{1,0:T(8,128)S(1)}, u32[]{:S(2)}, u32[]{:S(2)}) collective-permute-start(f32[16,1182]{1,0:T(8,128)S(1)} %collective-permute-done.16), channel_id=1, source_target_pairs={{16,0},{32,16},{48,32},{64,48},{80,64},{96,80},{112,96},{128,112},... | collective-permute-start | bytes 226952 | tf_op jit(solution)/shard_map/ppermute | solution.py:25
  1594.5 16.1 collective-permute-start.11
  1600.2 20.6 %copy-start.1 = (s32[1,272]{1,0:T(1,128)S(1)}, s32[1,272]{1,0:T(1,128)}, u32[]{:S(2)}) copy-start(s32[1,272]{1,0:T(1,128)} %param.9) | copy-start | bytes 3268
  1610.6 7.8 collective-permute-start.18
Sparse Core Ops, SparseCore 0:
  10.9 62.2 all-gather.1
  229.3 1277.4 reduce-scatter.1
